TPU v7x, 256 devices: a whole 4x4x8 slice. The times are simulated.
256 devices in a mesh: shard: 16 (over y, z_hi, core), rep: 16 (over x, z_lo).
Axes of the slice: x: 4, y: 4, z: 8 (z_hi: 2, z_lo: 4; z = z_hi * 4 + z_lo), core: 2. Of those that a mesh axis runs over, the one named last changes fastest.
Arguments:
- inputs: bfloat16 [50432, 768], P(('shard', 'rep')), may hold values from -6 to 6
- norm1_gain: float32 [768], replicated, may hold values from 0.25 to 1.75
- w_qkv: bfloat16 [768, 2304], P('shard'), may hold values from -0.21875 to 0.21875
- w_proj: bfloat16 [768, 768], P('shard'), may hold values from -0.875 to 0.875
- norm2_gain: float32 [768], replicated, may hold values from 0.25 to 1.75
- w_router: bfloat16 [768, 32], P('shard'), may hold values from -0.21875 to 0.21875
- w_expert_in: bfloat16 [2, 768, 3072], P(None, 'shard'), may hold values from -0.21875 to 0.21875
- w_expert_out: bfloat16 [2, 3072, 768], P(None, 'shard'), may hold values from -0.875 to 0.875
- expert_ids: int32 [50432, 2], P(('shard', 'rep')), may hold values from 0 to 1, all different within a row
- capacity: int32 [2], replicated, may hold values from 64 to 128, as said below
- cotangent: bfloat16 [50432, 768], P(('shard', 'rep')), may hold values from -6 to 6
Outputs:
- outputs: bfloat16 [50432, 768], P(('shard', 'rep'))
- grad_inputs: float32 [50432, 768], P(('shard', 'rep'))
- grad_norm1_gain: float32 [768], replicated
- grad_qkv: float32 [768, 2304], P('shard')
- grad_proj: float32 [768, 768], P('shard')
- grad_norm2_gain: float32 [768], replicated
- grad_router: float32 [768, 32], P('shard')
- grad_expert_in: float32 [2, 768, 3072], P(None, 'shard')
- grad_expert_out: float32 [2, 3072, 768], P(None, 'shard')
Inputs may be any that keep to these rules, and one draw needn't show every extreme that they name: Every expert's capacity is 64 to 128; some expert has exactly 128. `expert_ids`: the two experts of a token differ.
All inputs are finite; a program needn't handle non-finite values.
Results may differ from a plain program's by a relative error of at most 0.025.
Values may be sent and summed in bfloat16 or wider, within the bound.
No kernel may reach another device: no remote copies, remote signals or barrier semaphores. Data moves between devices by JAX's collectives and lax.ppermute only.
A program may use at most 128 MiB of HBM per device.

v0:
```python
import jax
import jax.numpy as jnp
from jax import lax
from jax.sharding import PartitionSpec as P

HEADS = 12
HD = 64
EXPERTS = 32
E_WIN = 2
SEQ = 197
CAP = 128
EPS = 1e-06


def layer_norm(values, gain):
    centred = values - jnp.mean(values, axis=-1, keepdims=True)
    inverse = lax.rsqrt(jnp.mean(centred * centred, axis=-1, keepdims=True) + EPS)
    normed = centred * inverse
    return (normed, inverse, (normed * gain).astype(jnp.bfloat16))


def layer_norm_back(grad_out, normed, inverse, gain):
    scaled = grad_out * gain
    grad_in = inverse * (
        scaled
        - jnp.mean(scaled, axis=-1, keepdims=True)
        - normed * jnp.mean(scaled * normed, axis=-1, keepdims=True)
    )
    return (grad_in, jnp.sum(grad_out * normed, axis=0))


def heads_view(block, images):
    return block.reshape(images, SEQ, HEADS, HD)


def attention_scores(qkv, images):
    width = HEADS * HD
    query = heads_view(qkv[:, :width], images)
    keys = heads_view(qkv[:, width : 2 * width], images)
    values = heads_view(qkv[:, 2 * width :], images)
    scores = jnp.einsum(
        "bqhd,bkhd->bhqk", query, keys, preferred_element_type=jnp.float32
    ) * HD ** (-0.5)
    return (query, keys, values, scores)


def attention_forward(qkv, images):
    query, keys, values, scores = attention_scores(qkv, images)
    logsum = jax.nn.logsumexp(scores, axis=-1, keepdims=True)
    probs = jnp.exp(scores - logsum).astype(jnp.bfloat16)
    mixed = jnp.einsum("bhqk,bkhd->bqhd", probs, values, preferred_element_type=jnp.float32).astype(
        jnp.bfloat16
    )
    return (mixed.reshape(images * SEQ, HEADS * HD), logsum)


def attention_backward(qkv, mixed, logsum, grad_mixed, images):
    query, keys, values, scores = attention_scores(qkv, images)
    probs_full = jnp.exp(scores - logsum)
    probs = probs_full.astype(jnp.bfloat16)
    grad_out = heads_view(grad_mixed, images)
    out_rows = heads_view(mixed, images)
    grad_values = jnp.einsum("bhqk,bqhd->bkhd", probs, grad_out, preferred_element_type=jnp.float32)
    grad_probs = jnp.einsum("bqhd,bkhd->bhqk", grad_out, values, preferred_element_type=jnp.float32)
    delta = jnp.sum(grad_out.astype(jnp.float32) * out_rows.astype(jnp.float32), axis=-1)
    delta = jnp.transpose(delta, (0, 2, 1))[..., None]
    grad_scores = (probs_full * (grad_probs - delta)).astype(jnp.bfloat16)
    scale = HD ** (-0.5)
    grad_query = (
        jnp.einsum("bhqk,bkhd->bqhd", grad_scores, keys, preferred_element_type=jnp.float32) * scale
    )
    grad_keys = (
        jnp.einsum("bhqk,bqhd->bkhd", grad_scores, query, preferred_element_type=jnp.float32)
        * scale
    )
    width = HEADS * HD
    rows = images * SEQ
    return jnp.concatenate(
        [
            grad_query.reshape(rows, width),
            grad_keys.reshape(rows, width),
            grad_values.reshape(rows, width),
        ],
        axis=1,
    ).astype(jnp.bfloat16)


def route_masks(expert_ids, capacity):
    count = expert_ids.shape[0]
    picked_hot = (expert_ids[:, :, None] == jnp.arange(E_WIN)[None, None, :]).astype(jnp.int32)
    ordered = jnp.transpose(picked_hot, (1, 0, 2)).reshape(2 * count, E_WIN)
    before = jnp.cumsum(ordered, axis=0) - ordered
    position = jnp.sum(before * ordered, axis=1).reshape(2, count).T
    limit = jnp.sum(picked_hot * capacity[None, None, :], axis=2)
    kept_mask = (position < limit).astype(jnp.float32)
    slot_hot = (position[:, :, None] == jnp.arange(CAP)[None, None, :]).astype(jnp.float32)
    return (
        kept_mask[:, :, None, None]
        * picked_hot.astype(jnp.float32)[:, :, :, None]
        * slot_hot[:, :, None, :]
    )


def body(
    inputs,
    norm1_gain,
    w_qkv,
    w_proj,
    norm2_gain,
    w_router,
    w_expert_in,
    w_expert_out,
    expert_ids,
    capacity,
    cotangent,
):
    high = lax.Precision.HIGHEST
    images = inputs.shape[0] // SEQ
    shard_rows = w_qkv.shape[0]
    hid_rows = w_expert_out.shape[1]
    full_qkv, full_proj, full_router = (
        lax.all_gather(w_qkv, "shard", axis=0, tiled=True),
        lax.all_gather(w_proj, "shard", axis=0, tiled=True),
        lax.all_gather(w_router, "shard", axis=0, tiled=True),
    )
    x_float = inputs.astype(jnp.float32)
    normed1, inverse1, hidden1 = layer_norm(x_float, norm1_gain)
    qkv = jnp.dot(hidden1, full_qkv, preferred_element_type=jnp.float32).astype(jnp.bfloat16)
    mixed, logsum = attention_forward(qkv, images)
    attended = x_float + jnp.dot(mixed, full_proj, preferred_element_type=jnp.float32)
    normed2, inverse2, hidden2 = layer_norm(attended, norm2_gain)
    logits = jnp.dot(hidden2, full_router, preferred_element_type=jnp.float32)
    router = jax.nn.softmax(logits, axis=-1)
    expert_hot = (expert_ids[:, :, None] == jnp.arange(EXPERTS)[None, None, :]).astype(jnp.float32)
    gate = jnp.sum(router[:, None, :] * expert_hot, axis=2)
    masks = route_masks(expert_ids, capacity)
    dispatch_float = jnp.sum(masks, axis=1)
    dispatch = dispatch_float.astype(jnp.bfloat16)
    combine = jnp.sum(masks * gate[:, :, None, None], axis=1)
    expert_rows = jnp.einsum(
        "rec,rd->ecd", dispatch, hidden2, preferred_element_type=jnp.float32
    ).astype(jnp.bfloat16)
    kept_weights = []
    pre_list = []
    activated_list = []
    eout_list = []
    for expert in range(E_WIN):
        first, second = (
            lax.all_gather(w_expert_in[expert], "shard", axis=0, tiled=True),
            lax.all_gather(w_expert_out[expert], "shard", axis=0, tiled=True),
        )
        kept_weights.append((first, second))
        pre = jnp.dot(expert_rows[expert], first, preferred_element_type=jnp.float32)
        activated = jax.nn.gelu(pre, approximate=False).astype(jnp.bfloat16)
        pre_list.append(pre)
        activated_list.append(activated)
        eout_list.append(
            jnp.dot(activated, second, preferred_element_type=jnp.float32).astype(jnp.bfloat16)
        )
    expert_out = jnp.stack(eout_list)
    eout_float = expert_out.astype(jnp.float32)
    moe = jnp.einsum("rec,ecd->rd", combine, eout_float, precision=high)
    outputs = (attended + moe).astype(jnp.bfloat16)
    grad = cotangent.astype(jnp.float32)
    matched = jnp.einsum("rd,ecd->rec", grad, eout_float, precision=high)
    grad_gate = jnp.sum(masks * matched[:, None, :, :], axis=(2, 3))
    grad_eout = jnp.einsum("rec,rd->ecd", combine, grad, precision=high).astype(jnp.bfloat16)
    back_qkv, back_proj, back_router = (full_qkv, full_proj, full_router)
    in_list = []
    out_list = []
    grad_rows_list = []
    for expert in range(E_WIN):
        first, second = kept_weights[expert]
        pre = pre_list[expert]
        grad_act = jnp.einsum(
            "cd,hd->ch", grad_eout[expert], second, preferred_element_type=jnp.float32
        )
        slope = (
            0.5 * (1.0 + jax.scipy.special.erf(pre * 0.7071067811865476))
            + pre * jnp.exp(-0.5 * pre * pre) * 0.3989422804014327
        )
        grad_pre = (grad_act * slope).astype(jnp.bfloat16)
        grad_rows_list.append(
            jnp.einsum("ch,dh->cd", grad_pre, first, preferred_element_type=jnp.float32).astype(
                jnp.bfloat16
            )
        )
        rows_here = expert_rows[expert]
        act_here = activated_list[expert]
        eout_here = grad_eout[expert]

        def in_term(start, count, rows_here=rows_here, grad_pre=grad_pre):
            return jnp.einsum("cd,ch->dh", rows_here, grad_pre, preferred_element_type=jnp.float32)

        def out_term(start, count, act_here=act_here, eout_here=eout_here):
            return jnp.einsum("ch,cd->hd", act_here, eout_here, preferred_element_type=jnp.float32)

        in_list.append(
            lax.psum_scatter(
                in_term(jnp.int32(0), shard_rows * lax.axis_size("shard")).astype(jnp.bfloat16),
                "shard",
                scatter_dimension=0,
                tiled=True,
            ).astype(jnp.float32)
        )
        out_list.append(
            lax.psum_scatter(
                out_term(jnp.int32(0), hid_rows * lax.axis_size("shard")).astype(jnp.bfloat16),
                "shard",
                scatter_dimension=0,
                tiled=True,
            ).astype(jnp.float32)
        )
    grad_rows = jnp.stack(grad_rows_list)
    grad_probs = jnp.sum(grad_gate[:, :, None] * expert_hot, axis=1)
    grad_logits = (
        router * (grad_probs - jnp.sum(router * grad_probs, axis=-1, keepdims=True))
    ).astype(jnp.bfloat16)
    grad_hidden2 = jnp.einsum(
        "rec,ecd->rd", dispatch, grad_rows, preferred_element_type=jnp.float32
    ) + jnp.einsum("re,de->rd", grad_logits, back_router, preferred_element_type=jnp.float32)
    grad_norm2, gain2 = layer_norm_back(grad_hidden2, normed2, inverse2, norm2_gain)
    grad_attended = grad + grad_norm2
    grad_branch = grad_attended.astype(jnp.bfloat16)
    grad_mixed = jnp.einsum(
        "rk,dk->rd", grad_branch, back_proj, preferred_element_type=jnp.float32
    ).astype(jnp.bfloat16)
    grad_qkv_rows = attention_backward(qkv, mixed, logsum, grad_mixed, images)
    grad_hidden1 = jnp.einsum(
        "rk,dk->rd", grad_qkv_rows, back_qkv, preferred_element_type=jnp.float32
    )
    grad_norm1, gain1 = layer_norm_back(grad_hidden1, normed1, inverse1, norm1_gain)
    grad_inputs = grad_attended + grad_norm1
    gain1_total, gain2_total = lax.psum((gain1, gain2), ("shard", "rep"))
    dense_local = lax.psum_scatter(
        jnp.concatenate(
            [
                jnp.einsum("rc,rk->ck", hidden1, grad_qkv_rows, preferred_element_type=jnp.float32),
                jnp.einsum("rc,rk->ck", mixed, grad_branch, preferred_element_type=jnp.float32),
                jnp.einsum("rc,rk->ck", hidden2, grad_logits, preferred_element_type=jnp.float32),
            ],
            axis=1,
        ).astype(jnp.bfloat16),
        "shard",
        scatter_dimension=0,
        tiled=True,
    )
    dense_total, in_total, out_total = (
        lax.psum(dense_local, "rep").astype(jnp.float32),
        lax.psum(jnp.stack(in_list).astype(jnp.bfloat16), "rep").astype(jnp.float32),
        lax.psum(jnp.stack(out_list).astype(jnp.bfloat16), "rep").astype(jnp.float32),
    )
    width = HEADS * HD
    return (
        outputs,
        grad_inputs,
        gain1_total,
        dense_total[:, : 3 * width],
        dense_total[:, 3 * width : 4 * width],
        gain2_total,
        dense_total[:, 4 * width :],
        in_total,
        out_total,
    )


def solution(mesh):
    in_specs = (
        P(("shard", "rep"), None),
        P(),
        P("shard", None),
        P("shard", None),
        P(),
        P("shard", None),
        P(None, "shard", None),
        P(None, "shard", None),
        P(("shard", "rep"), None),
        P(),
        P(("shard", "rep"), None),
    )
    out_specs = (
        P(("shard", "rep"), None),
        P(("shard", "rep"), None),
        P(),
        P("shard", None),
        P("shard", None),
        P(),
        P("shard", None),
        P(None, "shard", None),
        P(None, "shard", None),
    )
    return jax.shard_map(body, mesh=mesh, in_specs=in_specs, out_specs=out_specs, check_vma=False)
```

profile of v0, /device:TPU:24, one launch (start us, length us, event | category | flops | bytes accessed | tf_op | source)
XLA Modules:
  0.0 1204.1 jit_solution(413905897846838815)
XLA Ops:
  8.0 0.7 all-gather.14.cloned.1.call-update
  8.7 1.9 fusion.130
  10.7 0.9 fusion.129
  14.3 31.0 %all-gather.4 = bf16[16,48,32]{1,2,0:T(8,128)(2,1)S(1)} all-gather(bf16[1,48,32]{1,2,0:T(8,128)(2,1)S(1)} %bitcast.199), channel_id=1, replica_groups=mesh['shard'=16,'rep'=16] {'shard'}, dimensions={0}, use_global_device_ids=true | all-gather | bytes 52224 | tf_op jit(solution)/shard_map/all_gather | solution.py:124
  45.4 0.8 reshape.247
  47.8 39.1 %all-gather.12.cloned.1.call-done = bf16[768,2304]{1,0:T(8,128)(2,1)} async-done(((bf16[48,2304]{1,0:T(8,128)(2,1)}), bf16[768,2304]{1,0:T(8,128)(2,1)}) %all-gather.12.cloned.1.call-update) | async-done | bytes 3538960 | tf_op jit(solution)/shard_map/all_gather | solution.py:122
  86.8 3.0 convolution_convert_fusion.5
  89.9 0.9 copy.108
  90.8 0.9 copy.107
  91.9 1.8 multiply_reduce_fusion
  94.3 1.4 convolution_convert_fusion.10
  95.6 46.1 %all-gather.14.cloned.1.call-done = bf16[768,768]{1,0:T(8,128)(2,1)} async-done(((bf16[48,768]{1,0:T(8,128)(2,1)}), bf16[768,768]{1,0:T(8,128)(2,1)}) %all-gather.14.cloned.1.call-update) | async-done | bytes 1179664 | tf_op jit(solution)/shard_map/all_gather | solution.py:123
  141.7 1.9 fusion.131
  144.6 0.7 copy-done.6
  146.3 1.4 copy.113
  147.7 2.0 convolution_convert_fusion.9
  149.7 72.3 %all-gather.20.cloned.1.call-done = bf16[1,768,3072]{2,1,0:T(8,128)(2,1)} async-done(((bf16[1,48,3072]{2,1,0:T(8,128)(2,1)}), bf16[1,768,3072]{2,1,0:T(8,128)(2,1)}) %all-gather.20.cloned.1.call-update) | async-done | bytes 4718608 | tf_op jit(solution)/shard_map/all_gather | solution.py:149
  222.0 7.7 fusion.34
  229.7 71.5 %all-gather.22.cloned.1.call-done = bf16[1,3072,768]{2,1,0:T(8,128)(2,1)} async-done(((bf16[1,192,768]{2,1,0:T(8,128)(2,1)}), bf16[1,3072,768]{2,1,0:T(8,128)(2,1)}) %all-gather.22.cloned.1.call-update) | async-done | bytes 4718608 | tf_op jit(solution)/shard_map/all_gather | solution.py:150
  301.2 4.0 fusion.73
  305.2 75.7 %all-gather.16.cloned.1.call-done = bf16[1,768,3072]{2,1,0:T(8,128)(2,1)} async-done(((bf16[1,48,3072]{2,1,0:T(8,128)(2,1)}), bf16[1,768,3072]{2,1,0:T(8,128)(2,1)}) %all-gather.16.cloned.1.call-update) | async-done | bytes 4718608 | tf_op jit(solution)/shard_map/all_gather | solution.py:149
  380.9 7.9 fusion.31
  388.8 71.3 %all-gather.18.cloned.1.call-done = bf16[1,3072,768]{2,1,0:T(8,128)(2,1)} async-done(((bf16[1,192,768]{2,1,0:T(8,128)(2,1)}), bf16[1,3072,768]{2,1,0:T(8,128)(2,1)}) %all-gather.18.cloned.1.call-update) | async-done | bytes 4718608 | tf_op jit(solution)/shard_map/all_gather | solution.py:150
  460.1 3.4 fusion.79
  464.7 7.0 fusion.100
  472.9 0.7 copy-done.23
  473.7 3.7 convolution_convert_fusion
  477.4 4.7 convolution_convert_fusion.1
  482.3 4.8 fusion.22
  487.1 0.9 copy-done.12
  488.0 3.7 convolution_convert_fusion.2
  491.9 5.0 fusion.25
  496.9 0.9 copy-done.14
  497.8 3.5 convolution_convert_fusion.3
  501.4 1.6 copy.119
  503.7 4.3 fusion.82
  508.1 4.1 fusion.76
  513.4 0.8 copy-done
  514.2 1.3 convolution_convert_fusion.11
  515.5 1.9 copy.120
  517.4 2.0 copy.121
  519.4 1.1 convolution_convert_fusion.12
  520.6 0.8 copy.127
  521.4 1.4 multiply_reduce_fusion.1
  522.8 1.9 multiply_convert_fusion
  527.9 1.3 convolution_convert_fusion.4
  529.2 2.4 pad_maximum_fusion
  531.7 49.8 %reduce-scatter.14.cloned.1.call-done = bf16[192,768]{1,0:T(8,128)(2,1)} async-done(((bf16[3072,768]{1,0:T(8,128)(2,1)}), bf16[192,768]{1,0:T(8,128)(2,1)}) %reduce-scatter.14.cloned.1.call-update) | async-done | bytes 294928 | tf_op jit(solution)/shard_map/reduce_scatter | solution.py:207
  581.5 109.2 %reduce-scatter.12.cloned.1.call-done = bf16[192,768]{1,0:T(8,128)(2,1)} async-done(((bf16[3072,768]{1,0:T(8,128)(2,1)}), bf16[192,768]{1,0:T(8,128)(2,1)}) %reduce-scatter.12.cloned.1.call-update) | async-done | bytes 294928 | tf_op jit(solution)/shard_map/reduce_scatter | solution.py:207
  690.7 1.9 pad_maximum_fusion.3
  692.6 106.6 %reduce-scatter.10.cloned.1.call-done = bf16[48,3072]{1,0:T(8,128)(2,1)} async-done(((bf16[768,3072]{1,0:T(8,128)(2,1)}), bf16[48,3072]{1,0:T(8,128)(2,1)}) %reduce-scatter.10.cloned.1.call-update) | async-done | bytes 294928 | tf_op jit(solution)/shard_map/reduce_scatter | solution.py:199
  799.3 109.0 %reduce-scatter.8.cloned.1.call-done = bf16[48,3072]{1,0:T(8,128)(2,1)} async-done(((bf16[768,3072]{1,0:T(8,128)(2,1)}), bf16[48,3072]{1,0:T(8,128)(2,1)}) %reduce-scatter.8.cloned.1.call-update) | async-done | bytes 294928 | tf_op jit(solution)/shard_map/reduce_scatter | solution.py:199
  908.3 1.9 pad_maximum_fusion.2
  910.2 108.5 %reduce-scatter.6.cloned.1.call-done = bf16[48,3104]{1,0:T(8,128)(2,1)} async-done(((bf16[768,3104]{1,0:T(8,128)(2,1)}), bf16[48,3104]{1,0:T(8,128)(2,1)}) %reduce-scatter.6.cloned.1.call-update) | async-done | bytes 298000 | tf_op jit(solution)/shard_map/reduce_scatter | solution.py:235
  1018.8 4.2 fusion.96
  1022.9 74.5 %all-reduce.1 = (f32[768]{0:T(1024)}, f32[768]{0:T(1024)}) all-reduce(f32[768]{0:T(1024)S(1)} %get-tuple-element.56, f32[768]{0:T(1024)S(1)} %get-tuple-element.54), channel_id=1, replica_groups=mesh['shard'=16,'rep'=16] {'shard','rep'}, use_global_device_ids=true, to_apply=%region_24.25 | all-reduce | flops 1536 | bytes 12288 | tf_op jit(solution)/shard_map/psum | solution.py:234
  1098.8 1.1 fusion.60
  1100.0 1.1 fusion.95
  1101.1 88.9 %all-reduce.5.cloned.1.call-done = (bf16[48,3104]{1,0:T(8,128)(2,1)}, bf16[2,48,3072]{2,1,0:T(8,128)(2,1)}, bf16[2,192,768]{2,1,0:T(8,128)(2,1)}) async-done(((bf16[48,3104]{1,0:T(8,128)(2,1)}, bf16[2,48,3072]{2,1,0:T(8,128)(2,1)}, bf16[2,192,768]{2,1,0:T(8,128)(2,1)}), (bf16[48,3104]{1,0:T(8,128)(2,1)}, bf16[2,48,3072]{2,1,0:T(8,128)(2,1)}, bf16[2,192,768]{2,1,0:T(8,128)(2,1)})) %all-reduce.5.cloned.1.call-update) | async-done | bytes 1477648 | tf_op jit(solution)/shard_map/psum | solution.py:249
  1189.9 0.8 slice.86
  1190.7 1.6 slice.85
  1192.3 1.7 slice.84
  1194.7 1.1 convert_element_type.191
  1195.8 1.1 convert_element_type.194
  (179 shorter events, 17.6 us)
Async XLA Ops:
  7.2 3.5 copy-start.33
  7.2 79.7 %all-gather.12.cloned.1.call-start = ((), (), s32[]{:S(2)}) async-start(), calls=%async_computation.5 | async-start | bytes 3760128 | tf_op jit(solution)/shard_map/all_gather | solution.py:122
  7.9 133.8 %all-gather.14.cloned.1.call-start = ((), (), s32[]{:S(2)}) async-start(), calls=%async_computation.6 | async-start | bytes 1253376 | tf_op jit(solution)/shard_map/all_gather | solution.py:123
  8.7 4.2 copy-start.43
  8.7 213.3 %all-gather.20.cloned.1.call-start = ((), (), s32[]{:S(2)}) async-start(), calls=%async_computation.14 | async-start | bytes 5013504 | tf_op jit(solution)/shard_map/all_gather | solution.py:149
  10.6 3.7 copy-start.52
  10.6 35.6 %copy-start.53 = (s32[2]{0:T(128)S(1)}, s32[2]{0:T(128)}, u32[]{:S(2)}) copy-start(s32[2]{0:T(128)} %param.20) | copy-start | bytes 28
  10.7 35.8 %copy-start.3 = (bf16[197,768]{1,0:T(8,128)(2,1)S(1)}, bf16[197,768]{1,0:T(8,128)(2,1)}, u32[]{:S(2)}) copy-start(bf16[197,768]{1,0:T(8,128)(2,1)} %param.11) | copy-start | bytes 907780
  10.7 290.5 %all-gather.22.cloned.1.call-start = ((), (), s32[]{:S(2)}) async-start(), calls=%async_computation.15 | async-start | bytes 5013504 | tf_op jit(solution)/shard_map/all_gather | solution.py:150
  11.6 75.2 %copy-start.45 = (f32[768]{0:T(1024)S(1)}, f32[768]{0:T(1024)}, u32[]{:S(2)}) copy-start(f32[768]{0:T(1024)} %param.12) | copy-start | bytes 9220
  11.6 369.3 %all-gather.16.cloned.1.call-start = ((), (), s32[]{:S(2)}) async-start(), calls=%async_computation.12 | async-start | bytes 5013504 | tf_op jit(solution)/shard_map/all_gather | solution.py:149
  12.2 447.9 %all-gather.18.cloned.1.call-start = ((), (), s32[]{:S(2)}) async-start(), calls=%async_computation.13 | async-start | bytes 5013504 | tf_op jit(solution)/shard_map/all_gather | solution.py:150
  12.8 568.7 %reduce-scatter.14.cloned.1.call-start = ((), (), s32[]{:S(2)}) async-start(), calls=%async_computation.11 | async-start | bytes 5013504 | tf_op jit(solution)/shard_map/reduce_scatter | solution.py:207
  46.5 43.3 %copy-start.19 = (f32[197,2,2]{2,1,0:T(2,128)}, f32[197,2,2]{2,1,0:T(2,128)S(1)}, u32[]{:S(2)}) copy-start(f32[197,2,2]{2,1,0:T(2,128)S(1)} %copy.110) | copy-start | bytes 9460
  46.6 43.2 %copy-start.46 = (f32[197]{0:T(256)}, f32[197]{0:T(256)S(1)}, u32[]{:S(2)}) copy-start(f32[197]{0:T(256)S(1)} %broadcast_multiply_fusion.5) | copy-start | bytes 2368
  46.9 42.9 %copy-start.50 = (f32[197]{0:T(256)}, f32[197]{0:T(256)S(1)}, u32[]{:S(2)}) copy-start(f32[197]{0:T(256)S(1)} %add_rsqrt_fusion.1) | copy-start | bytes 2368
  47.2 42.7 %copy-start.21 = (f32[197,2,128]{2,1,0:T(2,128)}, f32[197,2,128]{2,1,0:T(2,128)S(1)}, u32[]{:S(2)}) copy-start(f32[197,2,128]{2,1,0:T(2,128)S(1)} %compare_convert_fusion) | copy-start | bytes 605188
  91.9 2.3 copy-start.8
  95.6 48.8 %copy-start.44 = (f32[768]{0:T(1024)S(1)}, f32[768]{0:T(1024)}, u32[]{:S(2)}) copy-start(f32[768]{0:T(1024)} %param.15) | copy-start | bytes 9220
  141.7 3.6 copy-start.34
  144.6 0.7 copy-start.6
  460.1 3.4 copy-start.24
  460.1 3.4 copy-start.26
  460.1 3.9 copy-start.36
  463.6 8.1 copy-start.28
  463.6 1.0 copy-start.20
  463.6 1.1 copy-start.22
  463.6 10.1 copy-start.5
  471.7 0.7 copy-start.17
  472.9 0.8 copy-start.23
  477.4 213.4 %reduce-scatter.12.cloned.1.call-start = ((), (), s32[]{:S(2)}) async-start(), calls=%async_computation.10 | async-start | bytes 5013504 | tf_op jit(solution)/shard_map/reduce_scatter | solution.py:207
  482.2 317.1 %reduce-scatter.10.cloned.1.call-start = ((), (), s32[]{:S(2)}) async-start(), calls=%async_computation.9 | async-start | bytes 5013504 | tf_op jit(solution)/shard_map/reduce_scatter | solution.py:199
  482.2 5.7 copy-start.15
  487.1 0.9 copy-start.12
  491.6 416.7 %reduce-scatter.8.cloned.1.call-start = ((), (), s32[]{:S(2)}) async-start(), calls=%async_computation.8 | async-start | bytes 5013504 | tf_op jit(solution)/shard_map/reduce_scatter | solution.py:199
  491.9 5.9 copy-start.16
  496.9 0.9 copy-start.14
  501.4 517.3 %reduce-scatter.6.cloned.1.call-start = ((), (), s32[]{:S(2)}) async-start(), calls=%async_computation.7 | async-start | bytes 5222400 | tf_op jit(solution)/shard_map/reduce_scatter | solution.py:235
  503.7 4.3 copy-start.13
  508.1 4.4 copy-start.35
  508.1 4.4 copy-start.49
  512.2 1.0 copy-start.25
  512.5 1.8 copy-start.7
  513.4 0.8 copy-start
  522.7 1.9 copy-start.11
  524.7 1.0 copy-start.10
  524.7 1.3 copy-start.1
  524.7 1.3 copy-start.4
  525.7 2.1 copy-start.39
  526.1 1.8 copy-start.41
  526.1 1.1 copy-start.9
  527.2 0.7 copy-start.51
  527.8 1.4 copy-start.37
  527.9 1.3 copy-start.30
  531.6 658.3 %all-reduce.5.cloned.1.call-start = ((), (), s32[]{:S(2)}) async-start(), calls=%async_computation.16 | async-start | bytes 2973696 | tf_op jit(solution)/shard_map/psum | solution.py:249
  692.6 326.1 %copy-start.38 = (bf16[12,64,197]{2,1,0:T(8,128)(2,1)S(1)}, bf16[12,64,197]{2,1,0:T(8,128)(2,1)}, u32[]{:S(2)}) copy-start(bf16[12,64,197]{2,1,0:T(8,128)(2,1)} %copy-done.37) | copy-start | bytes 907780
  692.6 326.1 %copy-start.40 = (bf16[12,64,197]{2,1,0:T(8,128)(2,1)S(1)}, bf16[12,64,197]{2,1,0:T(8,128)(2,1)}, u32[]{:S(2)}) copy-start(bf16[12,64,197]{2,1,0:T(8,128)(2,1)} %copy-done.39) | copy-start | bytes 907780
  692.6 326.1 %copy-start.42 = (bf16[12,64,197]{2,1,0:T(8,128)(2,1)S(1)}, bf16[12,64,197]{2,1,0:T(8,128)(2,1)}, u32[]{:S(2)}) copy-start(bf16[12,64,197]{2,1,0:T(8,128)(2,1)} %copy-done.41) | copy-start | bytes 907780
  1018.7 80.1 %copy-start.18 = (f32[197,2,128]{2,1,0:T(2,128)S(1)}, f32[197,2,128]{2,1,0:T(2,128)}, u32[]{:S(2)}) copy-start(f32[197,2,128]{2,1,0:T(2,128)} %copy-done.17) | copy-start | bytes 605188
  1018.7 80.1 %copy-start.27 = (bf16[1,128,768]{2,1,0:T(8,128)(2,1)S(1)}, bf16[1,128,768]{2,1,0:T(8,128)(2,1)}, u32[]{:S(2)}) copy-start(bf16[1,128,768]{2,1,0:T(8,128)(2,1)} %fusion.73) | copy-start | bytes 589828
  1018.8 80.1 %copy-start.29 = (bf16[1,128,768]{2,1,0:T(8,128)(2,1)S(1)}, bf16[1,128,768]{2,1,0:T(8,128)(2,1)}, u32[]{:S(2)}) copy-start(bf16[1,128,768]{2,1,0:T(8,128)(2,1)} %copy-done.28) | copy-start | bytes 589828
  1022.9 77.1 %copy-start.2 = (f32[197,768]{1,0:T(8,128)S(1)}, f32[197,768]{1,0:T(8,128)}, u32[]{:S(2)}) copy-start(f32[197,768]{1,0:T(8,128)} %copy-done) | copy-start | bytes 1815556
  1189.9 4.8 copy-start.32
  1189.9 5.9 copy-start.31
  (2 other events, 1.2 us)
Sparse Core Ops, SparseCore 0:
  10.7 76.0 all-gather.11
  89.5 52.1 all-gather.13
  145.0 76.9 all-gather.19
  224.6 76.5 all-gather.21
  304.3 76.5 all-gather.15
  383.5 76.5 all-gather.17
  477.5 103.9 reduce-scatter.13
  586.5 104.1 reduce-scatter.11
  695.1 104.1 reduce-scatter.9
  804.1 104.1 reduce-scatter.7
  912.8 105.8 reduce-scatter.5
  1022.5 167.3 all-reduce.4
where the time goes:
time: 1210 us; the launch traced here: 1200 us
  waiting for transfers between devices  951 us (79%)
  blocking collectives  106 us (9%)
  matrix products  81.6 us (7%)
  local copies, waits for them, and re-layouts  26.4 us (2%)
  other arithmetic  24 us (2%)
  between operations  15.4 us (1%)
    reduce_scatter x2, waiting for transfers between devices, body(): lax.psum_scatter(in_term(jnp.int32(0), shard_rows * lax.axis_size('shard'...  216 us
    reduce_scatter x2, waiting for transfers between devices, body(): lax.psum_scatter(out_term(jnp.int32(0), hid_rows * lax.axis_size('shard')...  159 us
    all_gather x2, waiting for transfers between devices, body(): lax.all_gather(w_expert_in[expert], 'shard', axis=0, tiled=True)  148 us
    all_gather x2, waiting for transfers between devices, body(): lax.all_gather(w_expert_out[expert], 'shard', axis=0, tiled=True)  143 us
    reduce_scatter x1, waiting for transfers between devices, body(): lax.psum_scatter(jnp.concatenate([jnp.einsum('rc,rk->ck', hidden1, grad_q...  108 us
    psum x1, waiting for transfers between devices, body(): lax.psum(dense_local, 'rep').astype(jnp.float32)  88.9 us
    psum x1, blocking collectives, body(): gain1_total, gain2_total = lax.psum((gain1, gain2), ('shard', 'rep'))  74.5 us
    all_gather x1, waiting for transfers between devices, body(): lax.all_gather(w_proj, 'shard', axis=0, tiled=True)  46.1 us
  transfers between devices with their start and end apart: 12, of which 12 were waited for; matrix products, arithmetic and copies ran while one was open for 9% of the time, Pallas kernels for 0%

commit v1 on v0

--- a/solution.py
+++ b/solution.py
@@ -1,3 +1,4 @@
+import functools
 import jax
 import jax.numpy as jnp
 from jax import lax
@@ -10,6 +11,18 @@
 SEQ = 197
 CAP = 128
 EPS = 1e-06
+
+
+def _pack_ratios(sample, ax_name):
+    return jnp.concatenate(
+        jax.lax.all_to_all(
+            jnp.stack([sample for _ in range(jax.lax.psum(1, ax_name))], 0), ax_name, 0, 0
+        ),
+        axis=0,
+    )
+
+
+find_table = functools.partial(_pack_ratios, ax_name="shard")
 
 
 def layer_norm(values, gain):
@@ -146,7 +159,7 @@
     eout_list = []
     for expert in range(E_WIN):
         first, second = (
-            lax.all_gather(w_expert_in[expert], "shard", axis=0, tiled=True),
+            find_table(w_expert_in[expert]),
             lax.all_gather(w_expert_out[expert], "shard", axis=0, tiled=True),
         )
         kept_weights.append((first, second))

time: 1210 us -> 1180 us (0.975)
  waiting for transfers between devices: 951 us -> 789 us
  blocking collectives: 106 us -> 202 us
  starting transfers between devices: 0.69 us -> 27.8 us
    all_gather x2 -> x0, waiting for transfers between devices: 148 us -> none  [body(): lax.all_gather(w_expert_in[expert], 'shard', axis=0, tiled=True)]
    all_to_all x0 -> x2, waiting for transfers between devices: none -> 122 us  [_pack_ratios(): jax.lax.all_to_all(jnp.stack([sample for _ in range(jax.lax.psum(1, ax_na...]
    all_gather x1, blocking collectives: 31 us -> 128 us  [body(): lax.all_gather(w_router, 'shard', axis=0, tiled=True)]
    all_gather x2, waiting for transfers between devices: 143 us -> 93.6 us  [body(): lax.all_gather(w_expert_out[expert], 'shard', axis=0, tiled=True)]
    all_gather x1, waiting for transfers between devices: 46.1 us -> 0.01 us  [body(): lax.all_gather(w_proj, 'shard', axis=0, tiled=True)]
    all_gather x1, waiting for transfers between devices: 39.1 us -> 0.02 us  [body(): lax.all_gather(w_qkv, 'shard', axis=0, tiled=True)]
    all_to_all x0 -> x2, starting transfers between devices: none -> 27.2 us  [_pack_ratios(): jax.lax.all_to_all(jnp.stack([sample for _ in range(jax.lax.psum(1, ax_na...]
  transfers between devices with their start and end apart: 12 -> 12, of which waited for: 12 -> 9; matrix products, arithmetic and copies ran while one was open for 9% -> 9% of each run, Pallas kernels for 0% -> 0%
where the time goes in v1:
time: 1180 us; the launch traced here: 1170 us
  waiting for transfers between devices  789 us (67%)
  blocking collectives  202 us (17%)
  matrix products  80.7 us (7%)
  local copies, waits for them, and re-layouts  31.9 us (3%)
  starting transfers between devices  27.8 us (2%)
  other arithmetic  24 us (2%)
  between operations  15.4 us (1%)
    reduce_scatter x2, waiting for transfers between devices, body(): lax.psum_scatter(in_term(jnp.int32(0), shard_rows * lax.axis_size('shard'...  216 us
    reduce_scatter x2, waiting for transfers between devices, body(): lax.psum_scatter(out_term(jnp.int32(0), hid_rows * lax.axis_size('shard')...  159 us
    all_gather x1, blocking collectives, body(): lax.all_gather(w_router, 'shard', axis=0, tiled=True)  128 us
    all_to_all x2, waiting for transfers between devices, _pack_ratios(): jax.lax.all_to_all(jnp.stack([sample for _ in range(jax.lax.psum(1, ax_na...  122 us
    reduce_scatter x1, waiting for transfers between devices, body(): lax.psum_scatter(jnp.concatenate([jnp.einsum('rc,rk->ck', hidden1, grad_q...  108 us
    all_gather x2, waiting for transfers between devices, body(): lax.all_gather(w_expert_out[expert], 'shard', axis=0, tiled=True)  93.6 us
    psum x1, waiting for transfers between devices, body(): lax.psum(dense_local, 'rep').astype(jnp.float32)  88.8 us
    psum x1, blocking collectives, body(): gain1_total, gain2_total = lax.psum((gain1, gain2), ('shard', 'rep'))  74.5 us
  transfers between devices with their start and end apart: 12, of which 9 were waited for; matrix products, arithmetic and copies ran while one was open for 9% of the time, Pallas kernels for 0%

profile of v1, /device:TPU:24, one launch (start us, length us, event | category | flops | bytes accessed | tf_op | source)
XLA Modules:
  0.0 1171.6 jit_solution(16610136236871043938)
XLA Ops:
  8.7 1.1 slice_bitcast_fusion.1
  9.8 2.7 stack.50
  12.5 11.5 all-to-all-start.1
  24.0 0.8 fusion.113
  24.9 121.9 %all-to-all-done.1 = bf16[16,48,3072]{2,1,0:T(8,128)(2,1)} async-done(((bf16[16,48,3072]{2,1,0:T(8,128)(2,1)}), bf16[16,48,3072]{2,1,0:T(8,128)(2,1)}, u32[]{:S(2)}, u32[]{:S(2)}) %all-to-all-start.1) | async-done | bytes 4718624 | tf_op jit(solution)/shard_map/all_to_all | solution.py:18
  146.8 2.8 stack.48
  149.7 15.8 %all-to-all-start = ((bf16[16,48,3072]{2,1,0:T(8,128)(2,1)}), bf16[16,48,3072]{2,1,0:T(8,128)(2,1)}, u32[]{:S(2)}, u32[]{:S(2)}) async-start(bf16[16,48,3072]{2,1,0:T(8,128)(2,1)} %stack.48), calls=%async_computation | async-start | bytes 9437184 | tf_op jit(solution)/shard_map/all_to_all | solution.py:18
  167.8 127.9 %all-gather.2 = bf16[16,48,32]{1,2,0:T(8,128)(2,1)S(1)} all-gather(bf16[1,48,32]{1,2,0:T(8,128)(2,1)S(1)} %bitcast.187), channel_id=1, replica_groups=mesh['shard'=16,'rep'=16] {'shard'}, dimensions={0}, use_global_device_ids=true | all-gather | bytes 52224 | tf_op jit(solution)/shard_map/all_gather | solution.py:137
  295.8 0.8 reshape.255
  297.9 3.0 convolution_convert_fusion.5
  301.1 0.9 copy.107
  302.0 0.9 copy.108
  303.0 1.7 multiply_reduce_fusion
  305.2 1.4 convolution_convert_fusion.10
  306.5 2.1 fusion.114
  311.2 1.4 copy.113
  312.7 1.3 convolution_convert_fusion.9
  314.0 0.7 copy-done.15
  314.7 7.6 fusion.26
  322.3 26.3 %all-gather.14.cloned.1.call-done = bf16[1,3072,768]{2,1,0:T(8,128)(2,1)} async-done(((bf16[1,192,768]{2,1,0:T(8,128)(2,1)}), bf16[1,3072,768]{2,1,0:T(8,128)(2,1)}) %all-gather.14.cloned.1.call-update) | async-done | bytes 4718608 | tf_op jit(solution)/shard_map/all_gather | solution.py:163
  348.6 4.0 fusion.61
  352.7 7.8 fusion.23
  360.5 67.3 %all-gather.12.cloned.1.call-done = bf16[1,3072,768]{2,1,0:T(8,128)(2,1)} async-done(((bf16[1,192,768]{2,1,0:T(8,128)(2,1)}), bf16[1,3072,768]{2,1,0:T(8,128)(2,1)}) %all-gather.12.cloned.1.call-update) | async-done | bytes 4718608 | tf_op jit(solution)/shard_map/all_gather | solution.py:163
  427.8 3.4 fusion.64
  432.3 7.0 fusion.82
  440.6 0.7 copy-done.24
  441.4 3.7 convolution_convert_fusion
  445.1 4.8 convolution_convert_fusion.1
  450.0 4.8 fusion.14
  454.8 0.9 copy-done.12
  455.7 3.6 convolution_convert_fusion.2
  459.6 5.0 fusion.17
  464.6 0.9 copy-done.13
  465.5 3.5 convolution_convert_fusion.3
  469.1 1.6 copy.119
  471.4 4.3 fusion.60
  475.7 4.1 fusion.59
  481.1 0.8 copy-done
  481.9 1.3 convolution_convert_fusion.11
  483.2 1.9 copy.120
  485.0 2.0 copy.121
  487.1 1.1 convolution_convert_fusion.14
  488.2 0.8 copy.127
  489.0 1.4 multiply_reduce_fusion.1
  490.4 1.9 multiply_convert_fusion
  495.5 1.3 convolution_convert_fusion.4
  496.9 2.4 pad_maximum_fusion
  499.3 49.8 %reduce-scatter.14.cloned.1.call-done = bf16[192,768]{1,0:T(8,128)(2,1)} async-done(((bf16[3072,768]{1,0:T(8,128)(2,1)}), bf16[192,768]{1,0:T(8,128)(2,1)}) %reduce-scatter.14.cloned.1.call-update) | async-done | bytes 294928 | tf_op jit(solution)/shard_map/reduce_scatter | solution.py:220
  549.1 109.0 %reduce-scatter.12.cloned.1.call-done = bf16[192,768]{1,0:T(8,128)(2,1)} async-done(((bf16[3072,768]{1,0:T(8,128)(2,1)}), bf16[192,768]{1,0:T(8,128)(2,1)}) %reduce-scatter.12.cloned.1.call-update) | async-done | bytes 294928 | tf_op jit(solution)/shard_map/reduce_scatter | solution.py:220
  658.1 1.9 pad_maximum_fusion.3
  660.0 106.6 %reduce-scatter.10.cloned.1.call-done = bf16[48,3072]{1,0:T(8,128)(2,1)} async-done(((bf16[768,3072]{1,0:T(8,128)(2,1)}), bf16[48,3072]{1,0:T(8,128)(2,1)}) %reduce-scatter.10.cloned.1.call-update) | async-done | bytes 294928 | tf_op jit(solution)/shard_map/reduce_scatter | solution.py:212
  766.7 109.1 %reduce-scatter.8.cloned.1.call-done = bf16[48,3072]{1,0:T(8,128)(2,1)} async-done(((bf16[768,3072]{1,0:T(8,128)(2,1)}), bf16[48,3072]{1,0:T(8,128)(2,1)}) %reduce-scatter.8.cloned.1.call-update) | async-done | bytes 294928 | tf_op jit(solution)/shard_map/reduce_scatter | solution.py:212
  875.8 1.9 pad_maximum_fusion.2
  877.7 108.5 %reduce-scatter.6.cloned.1.call-done = bf16[48,3104]{1,0:T(8,128)(2,1)} async-done(((bf16[768,3104]{1,0:T(8,128)(2,1)}), bf16[48,3104]{1,0:T(8,128)(2,1)}) %reduce-scatter.6.cloned.1.call-update) | async-done | bytes 298000 | tf_op jit(solution)/shard_map/reduce_scatter | solution.py:248
  986.3 4.2 fusion.78
  990.5 74.5 %all-reduce.1 = (f32[768]{0:T(1024)}, f32[768]{0:T(1024)}) all-reduce(f32[768]{0:T(1024)S(1)} %get-tuple-element.56, f32[768]{0:T(1024)S(1)} %get-tuple-element.54), channel_id=1, replica_groups=mesh['shard'=16,'rep'=16] {'shard','rep'}, use_global_device_ids=true, to_apply=%region_24.25 | all-reduce | flops 1536 | bytes 12288 | tf_op jit(solution)/shard_map/psum | solution.py:247
  1066.3 1.1 fusion.52
  1067.5 1.1 fusion.77
  1068.6 88.8 %all-reduce.5.cloned.1.call-done = (bf16[48,3104]{1,0:T(8,128)(2,1)}, bf16[2,48,3072]{2,1,0:T(8,128)(2,1)}, bf16[2,192,768]{2,1,0:T(8,128)(2,1)}) async-done(((bf16[48,3104]{1,0:T(8,128)(2,1)}, bf16[2,48,3072]{2,1,0:T(8,128)(2,1)}, bf16[2,192,768]{2,1,0:T(8,128)(2,1)}), (bf16[48,3104]{1,0:T(8,128)(2,1)}, bf16[2,48,3072]{2,1,0:T(8,128)(2,1)}, bf16[2,192,768]{2,1,0:T(8,128)(2,1)})) %all-reduce.5.cloned.1.call-update) | async-done | bytes 1477648 | tf_op jit(solution)/shard_map/psum | solution.py:262
  1157.4 1.8 slice.90
  1159.2 1.6 slice.91
  1160.7 0.7 slice.92
  1162.1 1.1 convert_element_type.191
  1163.2 1.1 convert_element_type.194
  (181 shorter events, 18.4 us)
Async XLA Ops:
  7.2 290.7 %all-gather.8.cloned.1.call-start = ((), (), s32[]{:S(2)}) async-start(), calls=%async_computation.7 | async-start | bytes 3760128 | tf_op jit(solution)/shard_map/all_gather | solution.py:135
  7.9 298.6 %all-gather.10.cloned.1.call-start = ((), (), s32[]{:S(2)}) async-start(), calls=%async_computation.8 | async-start | bytes 1253376 | tf_op jit(solution)/shard_map/all_gather | solution.py:136
  12.5 11.5 copy-start.34
  12.5 134.3 %all-to-all-start.1 = ((bf16[16,48,3072]{2,1,0:T(8,128)(2,1)}), bf16[16,48,3072]{2,1,0:T(8,128)(2,1)}, u32[]{:S(2)}, u32[]{:S(2)}) async-start(bf16[16,48,3072]{2,1,0:T(8,128)(2,1)} %stack.50), calls=%async_computation.1 | async-start | bytes 9437184 | tf_op jit(solution)/shard_map/all_to_all | solution.py:18
  24.0 324.6 %all-gather.14.cloned.1.call-start = ((), (), s32[]{:S(2)}) async-start(), calls=%async_computation.15 | async-start | bytes 5013504 | tf_op jit(solution)/shard_map/all_gather | solution.py:163
  149.6 16.4 %copy-start.44 = (s32[197,2]{0,1:T(2,128)S(1)}, s32[197,2]{0,1:T(2,128)}, u32[]{:S(2)}) copy-start(s32[197,2]{0,1:T(2,128)} %param.19) | copy-start | bytes 4732
  149.6 17.9 %copy-start.54 = (s32[2]{0:T(128)S(1)}, s32[2]{0:T(128)}, u32[]{:S(2)}) copy-start(s32[2]{0:T(128)} %param.20) | copy-start | bytes 28
  149.6 18.2 %copy-start.53 = (bf16[48,32]{0,1:T(8,128)(2,1)S(1)}, bf16[48,32]{0,1:T(8,128)(2,1)}, u32[]{:S(2)}) copy-start(bf16[48,32]{0,1:T(8,128)(2,1)} %param.16) | copy-start | bytes 9220
  149.7 146.9 %copy-start.3 = (bf16[197,768]{1,0:T(8,128)(2,1)S(1)}, bf16[197,768]{1,0:T(8,128)(2,1)}, u32[]{:S(2)}) copy-start(bf16[197,768]{1,0:T(8,128)(2,1)} %param.11) | copy-start | bytes 907780
  149.7 203.0 %all-to-all-start = ((bf16[16,48,3072]{2,1,0:T(8,128)(2,1)}), bf16[16,48,3072]{2,1,0:T(8,128)(2,1)}, u32[]{:S(2)}, u32[]{:S(2)}) async-start(bf16[16,48,3072]{2,1,0:T(8,128)(2,1)} %stack.48), calls=%async_computation | async-start | bytes 9437184 | tf_op jit(solution)/shard_map/all_to_all | solution.py:18
  165.4 132.4 %copy-start.46 = (f32[768]{0:T(1024)S(1)}, f32[768]{0:T(1024)}, u32[]{:S(2)}) copy-start(f32[768]{0:T(1024)} %param.12) | copy-start | bytes 9220
  165.4 262.4 %all-gather.12.cloned.1.call-start = ((), (), s32[]{:S(2)}) async-start(), calls=%async_computation.14 | async-start | bytes 5013504 | tf_op jit(solution)/shard_map/all_gather | solution.py:163
  166.0 383.1 %reduce-scatter.14.cloned.1.call-start = ((), (), s32[]{:S(2)}) async-start(), calls=%async_computation.13 | async-start | bytes 5013504 | tf_op jit(solution)/shard_map/reduce_scatter | solution.py:220
  167.8 133.0 %copy-start.20 = (f32[197,2,2]{2,1,0:T(2,128)}, f32[197,2,2]{2,1,0:T(2,128)S(1)}, u32[]{:S(2)}) copy-start(f32[197,2,2]{2,1,0:T(2,128)S(1)} %copy.110) | copy-start | bytes 9460
  296.7 4.1 copy-start.47
  296.9 3.9 copy-start.51
  297.2 3.6 copy-start.22
  301.1 4.0 copy-start.8
  306.5 2.9 copy-start.45
  306.5 3.8 copy-start.35
  309.6 0.7 copy-start.6
  314.0 0.7 copy-start.15
  427.8 3.4 copy-start.25
  427.8 3.4 copy-start.27
  427.8 3.9 copy-start.37
  431.2 8.1 copy-start.29
  431.2 1.0 copy-start.21
  431.3 1.1 copy-start.23
  431.3 10.1 copy-start.5
  439.4 0.7 copy-start.18
  440.6 0.8 copy-start.24
  445.0 213.1 %reduce-scatter.12.cloned.1.call-start = ((), (), s32[]{:S(2)}) async-start(), calls=%async_computation.12 | async-start | bytes 5013504 | tf_op jit(solution)/shard_map/reduce_scatter | solution.py:220
  449.9 316.7 %reduce-scatter.10.cloned.1.call-start = ((), (), s32[]{:S(2)}) async-start(), calls=%async_computation.11 | async-start | bytes 5013504 | tf_op jit(solution)/shard_map/reduce_scatter | solution.py:212
  450.0 5.7 copy-start.16
  454.8 0.9 copy-start.12
  459.3 416.5 %reduce-scatter.8.cloned.1.call-start = ((), (), s32[]{:S(2)}) async-start(), calls=%async_computation.10 | async-start | bytes 5013504 | tf_op jit(solution)/shard_map/reduce_scatter | solution.py:212
  459.6 5.9 copy-start.17
  464.6 0.9 copy-start.13
  469.0 517.2 %reduce-scatter.6.cloned.1.call-start = ((), (), s32[]{:S(2)}) async-start(), calls=%async_computation.9 | async-start | bytes 5222400 | tf_op jit(solution)/shard_map/reduce_scatter | solution.py:248
  471.4 4.3 copy-start.14
  475.7 4.4 copy-start.36
  475.7 4.4 copy-start.50
  479.8 1.0 copy-start.26
  480.1 1.8 copy-start.7
  481.0 0.8 copy-start
  490.4 1.9 copy-start.10
  492.3 1.0 copy-start.11
  492.3 1.3 copy-start.1
  492.3 1.3 copy-start.4
  493.3 2.1 copy-start.40
  493.7 1.8 copy-start.42
  493.7 1.1 copy-start.9
  495.4 1.4 copy-start.38
  495.5 1.3 copy-start.31
  499.3 658.1 %all-reduce.5.cloned.1.call-start = ((), (), s32[]{:S(2)}) async-start(), calls=%async_computation.16 | async-start | bytes 2973696 | tf_op jit(solution)/shard_map/psum | solution.py:262
  660.0 326.2 %copy-start.39 = (bf16[12,64,197]{2,1,0:T(8,128)(2,1)S(1)}, bf16[12,64,197]{2,1,0:T(8,128)(2,1)}, u32[]{:S(2)}) copy-start(bf16[12,64,197]{2,1,0:T(8,128)(2,1)} %copy-done.38) | copy-start | bytes 907780
  660.0 326.2 %copy-start.41 = (bf16[12,64,197]{2,1,0:T(8,128)(2,1)S(1)}, bf16[12,64,197]{2,1,0:T(8,128)(2,1)}, u32[]{:S(2)}) copy-start(bf16[12,64,197]{2,1,0:T(8,128)(2,1)} %copy-done.40) | copy-start | bytes 907780
  660.0 326.2 %copy-start.43 = (bf16[12,64,197]{2,1,0:T(8,128)(2,1)S(1)}, bf16[12,64,197]{2,1,0:T(8,128)(2,1)}, u32[]{:S(2)}) copy-start(bf16[12,64,197]{2,1,0:T(8,128)(2,1)} %copy-done.42) | copy-start | bytes 907780
  986.3 80.1 %copy-start.19 = (f32[197,2,128]{2,1,0:T(2,128)S(1)}, f32[197,2,128]{2,1,0:T(2,128)}, u32[]{:S(2)}) copy-start(f32[197,2,128]{2,1,0:T(2,128)} %copy-done.18) | copy-start | bytes 605188
  986.3 80.1 %copy-start.28 = (bf16[1,128,768]{2,1,0:T(8,128)(2,1)S(1)}, bf16[1,128,768]{2,1,0:T(8,128)(2,1)}, u32[]{:S(2)}) copy-start(bf16[1,128,768]{2,1,0:T(8,128)(2,1)} %fusion.61) | copy-start | bytes 589828
  986.3 80.1 %copy-start.30 = (bf16[1,128,768]{2,1,0:T(8,128)(2,1)S(1)}, bf16[1,128,768]{2,1,0:T(8,128)(2,1)}, u32[]{:S(2)}) copy-start(bf16[1,128,768]{2,1,0:T(8,128)(2,1)} %copy-done.29) | copy-start | bytes 589828
  990.4 77.0 %copy-start.2 = (f32[197,768]{1,0:T(8,128)S(1)}, f32[197,768]{1,0:T(8,128)}, u32[]{:S(2)}) copy-start(f32[197,768]{1,0:T(8,128)} %copy-done) | copy-start | bytes 1815556
  1157.4 4.8 copy-start.33
  1157.4 5.9 copy-start.32
  (3 other events, 1.9 us)
Sparse Core Ops, SparseCore 0:
  10.7 102.4 all-gather.7
  115.9 106.8 all-gather.9
  226.0 122.5 all-gather.13
  351.2 76.5 all-gather.11
  445.2 103.9 reduce-scatter.13
  554.0 104.0 reduce-scatter.11
  662.5 104.1 reduce-scatter.9
  771.6 104.1 reduce-scatter.7
  880.3 105.8 reduce-scatter.5
  990.1 167.2 all-reduce.4
